TPU v7x, 32 devices: a whole 2x2x4 slice. The times are simulated.
32 devices in a mesh: short: 8 (over z, y), long: 4 (over x, core).
Axes of the slice: x: 2, y: 2, z: 4, core: 2. Of those that a mesh axis runs over, the one named last changes fastest.
Arguments:
- query: bfloat16 [32768, 8, 128], P(('long', 'short')), may hold values from -6 to 6
- key: bfloat16 [32768, 8, 128], P(('long', 'short')), may hold values from -6 to 6
- value: bfloat16 [32768, 8, 128], P(('long', 'short')), may hold values from -6 to 6
- level_weight: float32 [8, 20, 32768], P(None, None, ('long', 'short')), may hold values from 0.25 to 1.75
Outputs:
- attended: bfloat16 [32768, 8, 128], P(('long', 'short'))
All inputs are finite; a program needn't handle non-finite values.
Results may differ from a plain program's by a relative error of at most 0.0019.
Values sent between devices are 32-bit elements; how exact they have to be, the bound alone decides.
A program may use at most 128 MiB of HBM per device.

v0:
```python
import jax
import jax.numpy as jnp
from jax import lax
from jax.sharding import PartitionSpec as P

EPSILON = 1e-06


def from_partner(value, axis, stride):
    return lax.ppermute(value, axis, [(i, i ^ 1 << stride) for i in range(lax.axis_size(axis))])


def level_table(row_ids, col_ids, local_bits):
    differ = jnp.bitwise_xor(row_ids[:, None], col_ids[None, :])
    levels = jnp.zeros(differ.shape, jnp.int32)
    for bit_no in range(local_bits):
        levels = levels + (differ >= 1 << bit_no).astype(jnp.int32)
    return levels


def near_part(query, key, value, level_weight):
    length = query.shape[0]
    local_bits = length.bit_length() - 1
    block_rows = min(512, length)
    col_ids = jnp.arange(length, dtype=jnp.int32)
    outputs = []
    for row_start in range(0, length, block_rows):
        row_ids = row_start + jnp.arange(block_rows, dtype=jnp.int32)
        levels = level_table(row_ids, col_ids, local_bits)
        causal = col_ids[None, :] <= row_ids[:, None]
        scores = jnp.einsum(
            "thd,shd->hts",
            query[row_start : row_start + block_rows],
            key,
            preferred_element_type=jnp.float32,
        )
        mixing = jnp.zeros(scores.shape, jnp.float32)
        for level_no in range(local_bits + 1):
            chosen = jnp.where(levels == level_no, 1.0, 0.0).astype(jnp.float32)
            mixing = (
                mixing
                + chosen[None]
                * level_weight[:, level_no, row_start : row_start + block_rows][:, :, None]
            )
        weighted = jnp.where(causal[None], mixing * scores, 0.0).astype(jnp.bfloat16)
        outputs.append(
            jnp.einsum("hts,she->the", weighted, value, preferred_element_type=jnp.float32)
        )
    return jnp.concatenate(outputs, 0)


def per_device(query, key, value, level_weight):
    length = query.shape[0]
    local_bits = length.bit_length() - 1
    state = jnp.einsum("thd,the->hde", key, value, preferred_element_type=jnp.float32)
    short_bits = lax.axis_size("short").bit_length() - 1
    long_bits = lax.axis_size("long").bit_length() - 1
    short_pos = lax.axis_index("short")
    long_pos = lax.axis_index("long")
    group = state
    found = []
    for bit_no in range(short_bits):
        other = from_partner(group, "short", bit_no)
        found.append(jnp.where(short_pos >> bit_no & 1 == 1, other, 0.0))
        group = group + other
    near_buckets = jnp.stack(found, 0)
    outer = group
    found_far = []
    for bit_no in range(long_bits):
        other_far = from_partner(outer, "long", bit_no)
        found_far.append(jnp.where(long_pos >> bit_no & 1 == 1, other_far, 0.0))
        if bit_no + 1 < long_bits:
            outer = outer + other_far
    far_buckets = jnp.stack(found_far, 0)
    buckets = jnp.concatenate([near_buckets, far_buckets], 0)
    near = near_part(query, key, value, level_weight)
    bit_count = buckets.shape[0]
    products = jnp.einsum(
        "thd,bhde->bthe", query.astype(jnp.float32), buckets, precision=lax.Precision.HIGHEST
    )
    gains = jnp.transpose(
        level_weight[:, local_bits + 1 : local_bits + 1 + bit_count, :], (1, 2, 0)
    )
    total = near + jnp.sum(products * gains[..., None], 0)
    scale = lax.rsqrt(jnp.mean(total * total, -1, keepdims=True) + EPSILON)
    return (total * scale).astype(jnp.bfloat16)


def solution(mesh):
    return jax.shard_map(
        per_device,
        mesh=mesh,
        in_specs=(
            P(("long", "short"), None, None),
            P(("long", "short"), None, None),
            P(("long", "short"), None, None),
            P(None, None, ("long", "short")),
        ),
        out_specs=P(("long", "short"), None, None),
        check_vma=False,
    )
```

profile of v0, /device:TPU:3, one launch (start us, length us, event | category | flops | bytes accessed | tf_op | source)
XLA Modules:
  0.0 141.9 jit_solution(5845116410432469240)
XLA Ops:
  0.0 0.0 copy-start
  0.0 4.2 %copy.15 = bf16[1024,8,128]{0,2,1:T(8,128)(2,1)} copy(bf16[1024,8,128]{2,1,0:T(8,128)(2,1)} %param.5) | data formatting | bytes 4194304 | tf_op args[1]
  4.3 3.4 %fusion.23 = f32[8,128,128]{2,1,0:T(8,128)} fusion(bf16[1024,8,128]{0,2,1:T(8,128)(2,1)} %copy.15, bf16[1024,8,128]{2,1,0:T(8,128)(2,1)S(1)} %copy-done), kind=kOutput, calls=%fused_computation.59 | convolution fusion | flops 268435456 | bytes 4718592 | tf_op jit(solution)/shard_map/thd,the->hde/dot_general | solution.py:55
  7.7 1.2 collective-permute-start
  9.0 6.3 %compare_select_fusion.10 = (f32[512,1024]{1,0:T(8,128)S(1)}, f32[512,1024]{1,0:T(8,128)S(1)}, f32[512,1024]{1,0:T(8,128)S(1)}, f32[512,1024]{1,0:T(8,128)S(1)},...) fusion(s32[512]{0:T(512)S(1)} %iota_add_fusion), kind=kLoop, calls=%fused_computation.45 | loop fusion | flops 27262976 | bytes 23070720 | tf_op jit(solution)/shard_map/jit(_where)/select_n | solution.py:39
  15.2 0.4 iota_compare_fusion
  15.6 0.7 compare_select_fusion.11
  16.3 0.7 compare_select_fusion.13
  16.9 0.7 compare_select_fusion.15
  17.6 0.0 copy-start.7
  17.6 0.7 compare_select_fusion.17
  18.2 0.9 copy-done.7
  19.2 0.1 fusion.33
  19.3 23.2 %select_convert_fusion.clone.4 = bf16[8,512,1024]{2,1,0:T(8,128)(2,1)} fusion(bf16[1024,8,128]{0,2,1:T(8,128)(2,1)} %copy.15, f32[8,512]{1,0:T(8,128)S(1)} %get-tuple-element.28, f32[512,1024]{1,0:T(8,128)} %get-tuple-element.39, f32[8,512]{1,0:T(8,128)S(1)} %get-tuple-element.8, f32[512,1024]{1,0:T(8,128)} %get-tuple-element.38, ...), kind=kOutput, calls=%fused_computation.2.clone.clone.clone.1 | convolution fusion | flops 1174405120 | bytes 35307520 | tf_op jit(solution)/shard_map/thd,shd->hts/dot_general | solution.py:31
  42.5 0.4 compare_select_fusion.21
  43.0 0.1 iota_compare_fusion.1
  43.1 0.0 copy-start.2
  43.1 0.7 compare_select_fusion.19
  43.8 0.0 collective-permute-done
  43.8 1.3 add.1184
  45.1 1.4 collective-permute-start.1
  46.4 0.0 copy-done.2
  46.4 21.8 %select_convert_fusion.1.clone.2 = bf16[8,512,1024]{2,1,0:T(8,128)(2,1)} fusion(bf16[1024,8,128]{0,2,1:T(8,128)(2,1)S(1)} %copy-done.2, f32[8,512]{1,0:T(8,128)S(1)} %get-tuple-element.18, f32[512,1024]{1,0:T(8,128)S(1)} %get-tuple-element.40, f32[8,512]{1,0:T(8,128)S(1)} %get-tuple-element.19, f32[512,1024]{1,0:T(8,128)S(1)} %get-tuple-element.41, ...), kind=kOutput, calls=%fused_computation.3.clone.clone.clone | convolution fusion | flops 1174405120 | bytes 35307520 | tf_op jit(solution)/shard_map/thd,shd->hts/dot_general | solution.py:31
  68.2 0.0 collective-permute-done.1
  68.2 0.1 add.1185
  68.3 0.0 slice-start.1
  68.3 2.4 %collective-permute-start.2 = (f32[8,128,128]{2,1,0:T(8,128)S(1)}, f32[8,128,128]{2,1,0:T(8,128)S(1)}, u32[]{:S(2)}, u32[]{:S(2)}) collective-permute-start(f32[8,128,128]{2,1,0:T(8,128)S(1)} %add.1185), channel_id=1, source_target_pairs={{0,16},{4,20},{8,24},{12,28},{16,0},{20,4},{24,8},{28,12},{1,17},{... | collective-permute-start | bytes 1572872 | tf_op jit(solution)/shard_map/ppermute | solution.py:10
  70.7 7.0 %convolution_bitcast_fusion = f32[512,8,128]{2,0,1:T(8,128)} fusion(bf16[1024,8,128]{2,1,0:T(8,128)(2,1)S(1)} %copy-done, bf16[8,512,1024]{2,1,0:T(8,128)(2,1)} %select_convert_fusion.clone.4), kind=kOutput, calls=%fused_computation.57 | convolution fusion | flops 1073741824 | bytes 12582912 | tf_op jit(solution)/shard_map/hts,she->the/dot_general | solution.py:47
  77.8 16.5 %collective-permute-done.2 = f32[8,128,128]{2,1,0:T(8,128)S(1)} collective-permute-done((f32[8,128,128]{2,1,0:T(8,128)S(1)}, f32[8,128,128]{2,1,0:T(8,128)S(1)}, u32[]{:S(2)}, u32[]{:S(2)}) %collective-permute-start.2) | collective-permute-done | bytes 524320 | tf_op jit(solution)/shard_map/ppermute | solution.py:10
  94.3 0.1 add.1186
  94.3 0.6 collective-permute-start.3
  94.9 0.0 slice-done.1
  94.9 3.7 %convolution_bitcast_fusion.1 = f32[512,8,128]{2,0,1:T(8,128)} fusion(bf16[1024,8,128]{2,1,0:T(8,128)(2,1)S(1)} %copy-done, bf16[8,512,1024]{2,1,0:T(8,128)(2,1)S(1)} %bitcast.76), kind=kOutput, calls=%fused_computation.58 | convolution fusion | flops 1073741824 | bytes 12582912 | tf_op jit(solution)/shard_map/hts,she->the/dot_general | solution.py:47
  98.6 0.9 slice_bitcast_fusion
  99.6 0.1 copy.19
  99.7 0.0 collective-permute-done.3
  99.8 1.1 add.1187
  100.9 0.0 copy-start.8
  100.9 0.3 collective-permute-start.4
  101.3 1.3 bitcast_dynamic-update-slice_fusion.1
  102.6 11.8 %collective-permute-done.4 = f32[8,128,128]{2,1,0:T(8,128)S(1)} collective-permute-done((f32[8,128,128]{2,1,0:T(8,128)S(1)}, f32[8,128,128]{2,1,0:T(8,128)S(1)}, u32[]{:S(2)}, u32[]{:S(2)}) %collective-permute-start.4) | collective-permute-done | bytes 524320 | tf_op jit(solution)/shard_map/ppermute | solution.py:10
  114.4 12.0 %fusion = f32[1024,8,128]{0,2,1:T(8,128)} fusion(f32[5,1024,8]{1,0,2:T(8,128)S(1)} %copy.19, f32[5,8,128,128]{3,2,1,0:T(8,128)S(1)} %bitcast_dynamic-update-slice_fusion, bf16[1024,8,128,1]{2,1,0,3:T(8,128)(2,1)S(1)} %bitcast.77), kind=kOutput, calls=%fused_computation.1 | convolution fusion | flops 8062500864 | bytes 9076736 | tf_op jit(solution)/shard_map/thd,bhde->bthe/dot_general | solution.py:78
  126.4 5.4 %copy.20 = f32[1024,8,128]{2,0,1:T(8,128)} copy(f32[1024,8,128]{0,2,1:T(8,128)} %fusion) | data formatting | bytes 8388608 | tf_op jit(solution)/shard_map/reduce_sum | solution.py:84
  131.8 4.8 %multiply_reduce_fusion = f32[1024,8]{0,1:T(8,128)S(1)} fusion(f32[1024,8,128]{2,0,1:T(8,128)} %copy.20, f32[512,8,128]{2,0,1:T(8,128)} %convolution_bitcast_fusion, f32[512,8,128]{2,0,1:T(8,128)} %convolution_bitcast_fusion.1), kind=kLoop, calls=%fused_computation.6 | loop fusion | flops 4186112 | bytes 8421376 | tf_op jit(solution)/shard_map/reduce_sum | solution.py:85
  136.6 0.5 copy-done.3
  137.2 0.6 copy-done.4
  137.8 1.4 %multiply_convert_fusion = bf16[1024,8,128]{2,0,1:T(8,128)(2,1)S(1)} fusion(f32[1024,8]{0,1:T(8,128)S(1)} %add_rsqrt_fusion, f32[1024,8,128]{2,0,1:T(8,128)S(1)} %copy-done.1, f32[512,8,128]{2,0,1:T(8,128)S(1)} %copy-done.3, f32[512,8,128]{2,0,1:T(8,128)S(1)} %copy-done.4), kind=kLoop, calls=%fused_computation.5 | loop fusion | flops 4194304 | bytes 10518528 | tf_op jit(solution)/shard_map/convert_element_type | solution.py:86
  139.2 2.7 %copy.21 = bf16[1024,8,128]{2,1,0:T(8,128)(2,1)} copy(bf16[1024,8,128]{2,0,1:T(8,128)(2,1)S(1)} %multiply_convert_fusion) | data formatting | bytes 4194304 | tf_op jit(solution)/shard_map/convert_element_type | solution.py:86
  (23 shorter events, 0.2 us)
Async XLA Ops:
  0.0 4.3 %copy-start = (bf16[1024,8,128]{2,1,0:T(8,128)(2,1)S(1)}, bf16[1024,8,128]{2,1,0:T(8,128)(2,1)}, u32[]{:S(2)}) copy-start(bf16[1024,8,128]{2,1,0:T(8,128)(2,1)} %param.6) | copy-start | bytes 6291460
  4.3 4.7 %copy-start.9 = (f32[8,20,1024]{2,0,1:T(8,128)S(1)}, f32[8,20,1024]{2,0,1:T(8,128)}, u32[]{:S(2)}) copy-start(f32[8,20,1024]{2,0,1:T(8,128)} %param.7) | copy-start | bytes 1966084
  7.7 36.1 %collective-permute-start = (f32[8,128,128]{2,1,0:T(8,128)}, f32[8,128,128]{2,1,0:T(8,128)}, u32[]{:S(2)}, u32[]{:S(2)}) collective-permute-start(f32[8,128,128]{2,1,0:T(8,128)} %fusion.23), channel_id=1, source_target_pairs={{0,4},{4,0},{8,12},{12,8},{16,20},{20,16},{24,28},{28,24},{1,5},{5... | collective-permute-start | bytes 1572872 | tf_op jit(solution)/shard_map/ppermute | solution.py:10
  17.6 1.6 %copy-start.7 = (bf16[1024,8,128]{2,1,0:T(8,128)(2,1)S(1)}, bf16[1024,8,128]{2,1,0:T(8,128)(2,1)}, u32[]{:S(2)}) copy-start(bf16[1024,8,128]{2,1,0:T(8,128)(2,1)} %param.4) | copy-start | bytes 6291460
  43.1 3.3 %copy-start.2 = (bf16[1024,8,128]{0,2,1:T(8,128)(2,1)S(1)}, bf16[1024,8,128]{0,2,1:T(8,128)(2,1)}, u32[]{:S(2)}) copy-start(bf16[1024,8,128]{0,2,1:T(8,128)(2,1)} %copy.15) | copy-start | bytes 6291460
  45.1 23.2 %collective-permute-start.1 = (f32[8,128,128]{2,1,0:T(8,128)S(1)}, f32[8,128,128]{2,1,0:T(8,128)S(1)}, u32[]{:S(2)}, u32[]{:S(2)}) collective-permute-start(f32[8,128,128]{2,1,0:T(8,128)S(1)} %add.1184), channel_id=1, source_target_pairs={{0,8},{4,12},{8,0},{12,4},{16,24},{20,28},{24,16},{28,20},{1,9},{5... | collective-permute-start | bytes 1572872 | tf_op jit(solution)/shard_map/ppermute | solution.py:10
  68.2 26.7 %slice-start = ((s8[8388608]{0:T(1024)(128)(4,1)}), s8[4194304]{0:T(1024)(128)(4,1)S(1)}, s32[]{:S(2)}) async-start(s8[8388608]{0:T(1024)(128)(4,1)} %bitcast.75), calls=%async_computation | async-start | bytes 8388608
  68.3 26.6 %slice-start.1 = ((s8[8388608]{0:T(1024)(128)(4,1)}), s8[4194304]{0:T(1024)(128)(4,1)S(1)}, s32[]{:S(2)}) async-start(s8[8388608]{0:T(1024)(128)(4,1)} %bitcast.75), calls=%async_computation.1 | async-start | bytes 8388608
  68.3 25.9 %collective-permute-start.2 = (f32[8,128,128]{2,1,0:T(8,128)S(1)}, f32[8,128,128]{2,1,0:T(8,128)S(1)}, u32[]{:S(2)}, u32[]{:S(2)}) collective-permute-start(f32[8,128,128]{2,1,0:T(8,128)S(1)} %add.1185), channel_id=1, source_target_pairs={{0,16},{4,20},{8,24},{12,28},{16,0},{20,4},{24,8},{28,12},{1,17},{... | collective-permute-start | bytes 1572872 | tf_op jit(solution)/shard_map/ppermute | solution.py:10
  94.3 4.4 %copy-start.5 = (f32[8,128,128]{2,1,0:T(8,128)}, f32[8,128,128]{2,1,0:T(8,128)S(1)}, u32[]{:S(2)}) copy-start(f32[8,128,128]{2,1,0:T(8,128)S(1)} %collective-permute-done.2) | copy-start | bytes 1572868
  94.3 5.4 %collective-permute-start.3 = (f32[8,128,128]{2,1,0:T(8,128)S(1)}, f32[8,128,128]{2,1,0:T(8,128)}, u32[]{:S(2)}, u32[]{:S(2)}) collective-permute-start(f32[8,128,128]{2,1,0:T(8,128)S(1)} %add.1186), channel_id=1, source_target_pairs={{0,1},{1,0},{2,3},{3,2},{4,5},{5,4},{6,7},{7,6},{8,9},{9,8},{10,11... | collective-permute-start | bytes 1572872 | tf_op jit(solution)/shard_map/ppermute | solution.py:10
  99.6 1.7 %copy-start.6 = (f32[8,128,128]{2,1,0:T(8,128)S(1)}, f32[8,128,128]{2,1,0:T(8,128)}, u32[]{:S(2)}) copy-start(f32[8,128,128]{2,1,0:T(8,128)} %copy-done.5) | copy-start | bytes 1572868
  100.9 13.6 %copy-start.8 = (bf16[1024,8,128]{2,1,0:T(8,128)(2,1)S(1)}, bf16[1024,8,128]{2,1,0:T(8,128)(2,1)}, u32[]{:S(2)}) copy-start(bf16[1024,8,128]{2,1,0:T(8,128)(2,1)} %param.4) | copy-start | bytes 6291460
  100.9 13.5 %collective-permute-start.4 = (f32[8,128,128]{2,1,0:T(8,128)S(1)}, f32[8,128,128]{2,1,0:T(8,128)S(1)}, u32[]{:S(2)}, u32[]{:S(2)}) collective-permute-start(f32[8,128,128]{2,1,0:T(8,128)S(1)} %add.1187), channel_id=1, source_target_pairs={{0,2},{1,3},{2,0},{3,1},{4,6},{5,7},{6,4},{7,5},{8,10},{9,11},{10,... | collective-permute-start | bytes 1572872 | tf_op jit(solution)/shard_map/ppermute | solution.py:10
  131.8 4.8 %copy-start.1 = (f32[1024,8,128]{2,0,1:T(8,128)S(1)}, f32[1024,8,128]{2,0,1:T(8,128)}, u32[]{:S(2)}) copy-start(f32[1024,8,128]{2,0,1:T(8,128)} %copy.20) | copy-start | bytes 12582916
  131.8 5.3 %copy-start.3 = (f32[512,8,128]{2,0,1:T(8,128)S(1)}, f32[512,8,128]{2,0,1:T(8,128)}, u32[]{:S(2)}) copy-start(f32[512,8,128]{2,0,1:T(8,128)} %convolution_bitcast_fusion) | copy-start | bytes 6291460
  131.8 5.9 %copy-start.4 = (f32[512,8,128]{2,0,1:T(8,128)S(1)}, f32[512,8,128]{2,0,1:T(8,128)}, u32[]{:S(2)}) copy-start(f32[512,8,128]{2,0,1:T(8,128)} %convolution_bitcast_fusion.1) | copy-start | bytes 6291460
where the time goes:
time: 144 us; the launch traced here: 142 us
  matrix products  71.3 us (50%)
  waiting for transfers between devices  28.3 us (20%)
  other arithmetic  20.6 us (14%)
  local copies, waits for them, and re-layouts  15.6 us (11%)
  starting transfers between devices  5.86 us (4%)
    dot_general x2, matrix products, near_part(): jnp.einsum('thd,shd->hts', query[row_start:row_start + block_rows], key,...  45.1 us
    ppermute x5, waiting for transfers between devices, from_partner(): lax.ppermute(value, axis, [(i, i ^ 1 << stride) for i in range(lax.axis_s...  28.3 us
    dot_general x1, matrix products, per_device(): jnp.einsum('thd,bhde->bthe', query.astype(jnp.float32), buckets, precisio...  12 us
    dot_general x2, matrix products, near_part(): jnp.einsum('hts,she->the', weighted, value, preferred_element_type=jnp.fl...  10.8 us
    select_n x7, other arithmetic, near_part(): chosen = jnp.where(levels == level_no, 1.0, 0.0).astype(jnp.float32)  9.92 us
    unnamed x25, local copies, waits for them, and re-layouts  6.35 us
    ppermute x5, starting transfers between devices, from_partner(): lax.ppermute(value, axis, [(i, i ^ 1 << stride) for i in range(lax.axis_s...  5.86 us
    reduce_sum x1, local copies, waits for them, and re-layouts, per_device(): total = near + jnp.sum(products * gains[..., None], 0)  5.39 us
  transfers between devices with their start and end apart: 5, of which 2 were waited for; matrix products, arithmetic and copies ran while one was open for 49% of the time, Pallas kernels for 0%

commit v1 on v0

v1 whole, which is shorter than its diff:
```python
import functools

import jax
import jax.numpy as jnp
from jax import lax
from jax.experimental import pallas as pl
from jax.experimental.pallas import tpu as pltpu
from jax.sharding import PartitionSpec as P

EPSILON = 1e-06
TILE = 256
SUB = 128
MESH_ID = pl.DeviceIdType.MESH


def log2(n):
    return n.bit_length() - 1


def flipped(bit, by):
    if isinstance(by, int):
        return 1 - bit if by else bit
    return bit + by - 2 * bit * by


def subsets(bits):
    found = []
    for mask in range(1, 1 << len(bits)):
        found.append(tuple(b for i, b in enumerate(bits) if mask >> i & 1))
    found.sort(key=lambda s: (len(s), [-b for b in reversed(s)]))
    return found


def nt_dot(a, b):
    return lax.dot_general(a, b, (((1,), (1,)), ((), ())), preferred_element_type=jnp.float32)


def kernel(
    short_bits, long_bits, heads, length, width,
    q_ref, k_ref, v_ref, w_ref, out_ref,
    wide_a, wide_b, q_heads, k_heads, v_turned, near, levels, sums, buckets, send_sem, recv_sem,
):
    bits = short_bits + long_bits
    rows = heads * width
    local_bits = log2(length)
    short_pos = lax.axis_index("short")
    long_pos = lax.axis_index("long")
    bit = [(short_pos // (1 << b)) % 2 for b in range(short_bits)]
    bit += [(long_pos // (1 << b)) % 2 for b in range(long_bits)]

    def partner(b):
        if b < short_bits:
            return {"short": short_pos + (1 - 2 * bit[b]) * (1 << b)}
        return {"long": long_pos + (1 - 2 * bit[b]) * (1 << b - short_bits)}

    def split_of(b):
        return list(range(min(b, short_bits))) if b >= 2 else []

    def piece(b, flips):
        split = split_of(b)
        start = 0
        for i, s in enumerate(split):
            start = start + (rows >> i + 1) * flipped(bit[s], 1 if s in flips else 0)
        size = rows >> len(split)
        return pl.ds(pl.multiple_of(start, 8), size)

    number = {}
    for b in range(2):
        number[b] = b * heads
    count = 2 * heads
    for b in range(2, bits):
        for key in [()] + subsets(split_of(b)):
            number[b, key] = count
            count += 1

    def copy(src, dst, where, no, to):
        return pltpu.make_async_remote_copy(
            src_ref=src.at[where], dst_ref=dst.at[where],
            send_sem=send_sem.at[no], recv_sem=recv_sem.at[no],
            device_id=partner(to), device_id_type=MESH_ID,
        )

    barrier = pltpu.get_barrier_semaphore()
    for b in range(bits):
        pl.semaphore_signal(barrier, inc=1, device_id=partner(b), device_id_type=MESH_ID)

    part = 64

    def widen(src, dst):
        def step(i, _):
            at = pl.multiple_of(i * part, part)
            x = src[pl.ds(at, part)].astype(jnp.float32)
            dst[pl.ds(pl.multiple_of(at * heads, part * heads), part * heads), :] = x.reshape(part * heads, width)
            return 0
        lax.fori_loop(0, length // part, step, 0)

    def head_chunk(i, flip0, flip1):
        i0 = i % (heads // 4)
        i1 = (i // (heads // 4)) % 2
        i2 = i // (heads // 2)
        h0 = flipped(bit[0], flipped(i2, flip0))
        h1 = flipped(bit[1], flipped(i1, flip1))
        return h0 * (heads // 2) + h1 * (heads // 4) + i0

    def rows_of(h):
        return pl.ds(pl.multiple_of(h * width, width), width)

    widen(k_ref, wide_a)
    widen(v_ref, wide_b)

    def state_step(i, _):
        h = head_chunk(i, 1, 1)
        key = wide_a[pl.ds(h, length, stride=heads), :].astype(jnp.bfloat16)
        turned = wide_b[pl.ds(h, length, stride=heads), :].T.astype(jnp.bfloat16)
        k_heads[h] = key
        v_turned[h] = turned
        where = rows_of(h)
        sums[0, where, :] = jnp.dot(turned, key, preferred_element_type=jnp.float32)

        @pl.when(i == 0)
        def _():
            pl.semaphore_wait(barrier, bits)

        copy(sums.at[0], buckets.at[0], where, number[0] + i, 0).start()
        return 0

    lax.fori_loop(0, heads, state_step, 0)

    row = lax.broadcasted_iota(jnp.int32, (SUB, SUB), 0)
    col = lax.broadcasted_iota(jnp.int32, (SUB, SUB), 1)
    differ = jnp.bitwise_xor(row, col)
    table = jnp.zeros((SUB, SUB), jnp.int32)
    for b in range(log2(SUB)):
        table = table + (differ >= 1 << b).astype(jnp.int32)
    levels[...] = jnp.where(row <= col, table, -1)

    widen(q_ref, wide_a)

    def near_head(h):
        q_heads[h] = wide_a[pl.ds(h, length, stride=heads), :].astype(jnp.bfloat16)
        level = levels[...]
        for ti in range(length // TILE):
            cols = pl.ds(ti * TILE, TILE)
            query = q_heads[h, cols, :]
            total = None
            for si in range(ti + 1):
                scores = nt_dot(k_heads[h, pl.ds(si * TILE, TILE), :], query)
                if si < ti:
                    weighted = scores * w_ref[h, pl.ds(log2(TILE) + (ti ^ si).bit_length(), 1), cols]
                else:
                    columns = []
                    for a in range(TILE // SUB):
                        at = pl.ds(ti * TILE + a * SUB, SUB)
                        parts = []
                        for c in range(TILE // SUB):
                            block = scores[c * SUB : (c + 1) * SUB, a * SUB : (a + 1) * SUB]
                            if c < a:
                                parts.append(block * w_ref[h, pl.ds(log2(SUB) + (a ^ c).bit_length(), 1), at])
                            elif c > a:
                                parts.append(jnp.zeros_like(block))
                            else:
                                mixing = jnp.zeros((SUB, SUB), jnp.float32)
                                for n in range(log2(SUB) + 1):
                                    mixing = jnp.where(level == n, w_ref[h, pl.ds(n, 1), at], mixing)
                                parts.append(mixing * block)
                        columns.append(jnp.concatenate(parts, 0))
                    weighted = jnp.concatenate(columns, 1)
                product = jnp.dot(
                    v_turned[h, :, pl.ds(si * TILE, TILE)], weighted.astype(jnp.bfloat16),
                    preferred_element_type=jnp.float32,
                )
                total = product if total is None else total + product
            near[h, :, cols] = total

    def received(b, key, where):
        copy(sums.at[b], buckets.at[b], where, number[b, key], b if not key else key[0]).wait_recv()

    def add_up(b, where):
        sums[b + 1, where, :] = sums[b, where, :] + buckets[b, where, :]

    def send_sums(b):
        c = copy(sums.at[b], buckets.at[b], piece(b, ()), number[b, ()], b)
        if b < bits - 1:
            c.start()
        else:
            pl.when(bit[b] == 0)(c.start)

    def pass_on(b, key):
        for g in split_of(b):
            if not key or g < key[0]:
                copy(buckets.at[b], buckets.at[b], piece(b, key), number[b, (g,) + key], g).start()

    def arrive(b):
        if b < bits - 1:
            received(b, (), piece(b, ()))
            add_up(b, piece(b + 1, ()))
            send_sums(b + 1)

            @pl.when(bit[b] == 1)
            def _():
                pass_on(b, ())
        else:
            @pl.when(bit[b] == 1)
            def _():
                received(b, (), piece(b, ()))
                pass_on(b, ())

    def gather(b):
        @pl.when(bit[b] == 1)
        def _():
            for key in subsets(split_of(b)):
                received(b, key, piece(b, key))
                pass_on(b, key)

    def step(i, _):
        near_head(i)
        where = rows_of(head_chunk(i, 0, 1))
        copy(sums.at[0], buckets.at[0], where, number[0] + i, 0).wait_recv()
        add_up(0, where)
        copy(sums.at[1], buckets.at[1], where, number[1] + i, 1).start()

        @pl.when(i == heads // 2)
        def _():
            for n in range(heads // 4):
                own = rows_of(head_chunk(n, 0, 0))
                copy(sums.at[1], buckets.at[1], own, number[1] + n, 1).wait_recv()
            add_up(1, piece(2, ()))
            send_sums(2)

        @pl.when(i == heads - 2)
        def _():
            arrive(2)
        return 0

    lax.fori_loop(0, heads, step, 0)
    for b in range(3, bits):
        arrive(b)

    def rest(n, _):
        own = rows_of(head_chunk(n, 0, 0))
        copy(sums.at[1], buckets.at[1], own, number[1] + n, 1).wait_recv()
        return 0

    lax.fori_loop(heads // 4, heads, rest, 0)
    for b in range(2, bits):
        gather(b)

    def far_head(h, _):
        where = rows_of(h)
        high = []
        low = []
        for b in range(bits):
            full = jnp.where(bit[b] == 1, buckets[b, where, :], 0.0)
            top = full.astype(jnp.bfloat16)
            high.append(top)
            low.append((full - top.astype(jnp.float32)).astype(jnp.bfloat16))
        both = jnp.concatenate([jnp.concatenate(high, 0), jnp.concatenate(low, 0)], 1)
        for ti in range(length // TILE):
            cols = pl.ds(ti * TILE, TILE)
            query = q_heads[h, cols, :]
            products = nt_dot(both, jnp.concatenate([query, query], 1))
            far = None
            for b in range(bits):
                term = products[b * width : (b + 1) * width] * w_ref[h, pl.ds(local_bits + 1 + b, 1), cols]
                far = term if far is None else far + term
            total = near[h, :, cols] + far
            scale = lax.rsqrt(jnp.mean(total * total, 0, keepdims=True) + EPSILON)
            wide_b[pl.ds(ti * TILE * heads + h, TILE, stride=heads), :] = (total * scale).T
        return 0

    lax.fori_loop(0, heads, far_head, 0)

    def narrow(i, _):
        at = pl.multiple_of(i * part, part)
        x = wide_b[pl.ds(pl.multiple_of(at * heads, part * heads), part * heads), :]
        out_ref[pl.ds(at, part)] = x.reshape(part, heads, width).astype(jnp.bfloat16)
        return 0

    lax.fori_loop(0, length // part, narrow, 0)

    def sent(i, _):
        copy(sums.at[0], buckets.at[0], rows_of(head_chunk(i, 1, 1)), number[0] + i, 0).wait_send()
        copy(sums.at[1], buckets.at[1], rows_of(head_chunk(i, 0, 1)), number[1] + i, 1).wait_send()
        return 0

    lax.fori_loop(0, heads, sent, 0)
    for b in range(2, bits):
        c = copy(sums.at[b], buckets.at[b], piece(b, ()), number[b, ()], b)
        if b < bits - 1:
            c.wait_send()
        else:
            pl.when(bit[b] == 0)(c.wait_send)

        @pl.when(bit[b] == 1)
        def _():
            for key in [()] + subsets(split_of(b)):
                for g in split_of(b):
                    if not key or g < key[0]:
                        copy(buckets.at[b], buckets.at[b], piece(b, key), number[b, (g,) + key], g).wait_send()


def per_device(query, key, value, level_weight):
    length, heads, width = query.shape
    short_bits = log2(lax.axis_size("short"))
    long_bits = log2(lax.axis_size("long"))
    bits = short_bits + long_bits
    rows = heads * width
    copies = 2 * heads + sum(1 << min(b, short_bits) for b in range(2, bits))
    vmem = pl.BlockSpec(memory_space=pltpu.VMEM)
    return pl.pallas_call(
        functools.partial(kernel, short_bits, long_bits, heads, length, width),
        out_shape=jax.ShapeDtypeStruct(query.shape, jnp.bfloat16),
        in_specs=[vmem] * 4,
        out_specs=vmem,
        scratch_shapes=[
            pltpu.VMEM((length * heads, width), jnp.float32),
            pltpu.VMEM((length * heads, width), jnp.float32),
            pltpu.VMEM((heads, length, width), jnp.bfloat16),
            pltpu.VMEM((heads, length, width), jnp.bfloat16),
            pltpu.VMEM((heads, width, length), jnp.bfloat16),
            pltpu.VMEM((heads, width, length), jnp.float32),
            pltpu.VMEM((SUB, SUB), jnp.int32),
            pltpu.VMEM((bits, rows, width), jnp.float32),
            pltpu.VMEM((bits, rows, width), jnp.float32),
            pltpu.SemaphoreType.DMA((copies,)),
            pltpu.SemaphoreType.DMA((copies,)),
        ],
        compiler_params=pltpu.CompilerParams(
            collective_id=0, has_side_effects=True, vmem_limit_bytes=60 * 1024 * 1024
        ),
    )(query, key, value, level_weight)


def solution(mesh):
    rows = P(("long", "short"), None, None)
    return jax.shard_map(
        per_device,
        mesh=mesh,
        in_specs=(rows, rows, rows, P(None, None, ("long", "short"))),
        out_specs=rows,
        check_vma=False,
    )
```

time: 144 us -> 56.8 us (0.39)
  the two profiles are of different devices: /device:TPU:3 before, /device:TPU:22 now
where the time goes in v1:
time: 56.8 us; the launch traced here: 56.6 us
  Pallas kernels  51.2 us (90%)
  local copies, waits for them, and re-layouts  5.4 us (10%)
    pallas_call x1, Pallas kernels, per_device(): pl.pallas_call(functools.partial(kernel, short_bits, long_bits, heads, le...  51.2 us
    unnamed x2, local copies, waits for them, and re-layouts  5.4 us

profile of v1, /device:TPU:22, one launch (start us, length us, event | category | flops | bytes accessed | tf_op | source)
XLA Modules:
  0.0 56.6 jit_solution(10207142760097695669)
XLA Ops:
  0.0 2.4 %copy.5.w_ref = f32[8,20,1024]{2,1,0:T(8,128)} copy(f32[8,20,1024]{2,0,1:T(8,128)} %param.7) | data formatting | bytes 1310720 | tf_op args[3]
  2.4 51.2 %shard_map.46 = bf16[1024,8,128]{2,1,0:T(8,128)(2,1)} custom-call(bf16[1024,8,128]{2,1,0:T(8,128)(2,1)} %q_ref.1, bf16[1024,8,128]{2,1,0:T(8,128)(2,1)} %k_ref.1, bf16[1024,8,128]{2,1,0:T(8,128)(2,1)} %v_ref.1, f32[8,20,1024]{2,1,0:T(8,128)} %copy.5.w_ref), custom_call_target="tpu_custom_call" | custom-call | tf_op jit(solution)/shard_map/pallas_call | solution.py:310
  53.5 3.0 %copy.7 = bf16[1024,8,128]{2,1,0:T(8,128)(2,1)} copy(bf16[1024,8,128]{2,1,0:T(8,128)(2,1)} %shard_map.46) | data formatting | bytes 4194304

commit v2 on v1

--- a/solution.py
+++ b/solution.py
@@ -38,7 +38,7 @@
 def kernel(
     short_bits, long_bits, heads, length, width,
     q_ref, k_ref, v_ref, w_ref, out_ref,
-    wide_a, wide_b, q_heads, k_heads, v_turned, near, levels, sums, buckets, send_sem, recv_sem,
+    k_in, v_in, q_in, w_in, wide_a, wide_b, q_heads, k_heads, v_turned, near, levels, sums, buckets, send_sem, recv_sem, load_sem,
 ):
     bits = short_bits + long_bits
     rows = heads * width
@@ -84,6 +84,15 @@
     for b in range(bits):
         pl.semaphore_signal(barrier, inc=1, device_id=partner(b), device_id_type=MESH_ID)
 
+    loads = [
+        pltpu.make_async_copy(src, dst, load_sem.at[n])
+        for n, (src, dst) in enumerate([(k_ref, k_in), (v_ref, v_in), (q_ref, q_in)])
+    ]
+    for h in range(heads):
+        loads.append(pltpu.make_async_copy(w_ref.at[:, h, :], w_in.at[h], load_sem.at[3 + h]))
+    for load in loads:
+        load.start()
+
     part = 64
 
     def widen(src, dst):
@@ -105,8 +114,10 @@
     def rows_of(h):
         return pl.ds(pl.multiple_of(h * width, width), width)
 
-    widen(k_ref, wide_a)
-    widen(v_ref, wide_b)
+    loads[0].wait()
+    widen(k_in, wide_a)
+    loads[1].wait()
+    widen(v_in, wide_b)
 
     def state_step(i, _):
         h = head_chunk(i, 1, 1)
@@ -134,7 +145,10 @@
         table = table + (differ >= 1 << b).astype(jnp.int32)
     levels[...] = jnp.where(row <= col, table, -1)
 
-    widen(q_ref, wide_a)
+    loads[2].wait()
+    widen(q_in, wide_a)
+    for load in loads[3:]:
+        load.wait()
 
     def near_head(h):
         q_heads[h] = wide_a[pl.ds(h, length, stride=heads), :].astype(jnp.bfloat16)
@@ -146,7 +160,7 @@
             for si in range(ti + 1):
                 scores = nt_dot(k_heads[h, pl.ds(si * TILE, TILE), :], query)
                 if si < ti:
-                    weighted = scores * w_ref[h, pl.ds(log2(TILE) + (ti ^ si).bit_length(), 1), cols]
+                    weighted = scores * w_in[h, pl.ds(log2(TILE) + (ti ^ si).bit_length(), 1), cols]
                 else:
                     columns = []
                     for a in range(TILE // SUB):
@@ -155,13 +169,13 @@
                         for c in range(TILE // SUB):
                             block = scores[c * SUB : (c + 1) * SUB, a * SUB : (a + 1) * SUB]
                             if c < a:
-                                parts.append(block * w_ref[h, pl.ds(log2(SUB) + (a ^ c).bit_length(), 1), at])
+                                parts.append(block * w_in[h, pl.ds(log2(SUB) + (a ^ c).bit_length(), 1), at])
                             elif c > a:
                                 parts.append(jnp.zeros_like(block))
                             else:
                                 mixing = jnp.zeros((SUB, SUB), jnp.float32)
                                 for n in range(log2(SUB) + 1):
-                                    mixing = jnp.where(level == n, w_ref[h, pl.ds(n, 1), at], mixing)
+                                    mixing = jnp.where(level == n, w_in[h, pl.ds(n, 1), at], mixing)
                                 parts.append(mixing * block)
                         columns.append(jnp.concatenate(parts, 0))
                     weighted = jnp.concatenate(columns, 1)
@@ -205,15 +219,13 @@
                 received(b, (), piece(b, ()))
                 pass_on(b, ())
 
-    def gather(b):
+    def gather(b, key):
         @pl.when(bit[b] == 1)
         def _():
-            for key in subsets(split_of(b)):
-                received(b, key, piece(b, key))
-                pass_on(b, key)
+            received(b, key, piece(b, key))
+            pass_on(b, key)
 
     def step(i, _):
-        near_head(i)
         where = rows_of(head_chunk(i, 0, 1))
         copy(sums.at[0], buckets.at[0], where, number[0] + i, 0).wait_recv()
         add_up(0, where)
@@ -227,14 +239,10 @@
             add_up(1, piece(2, ()))
             send_sums(2)
 
-        @pl.when(i == heads - 2)
-        def _():
-            arrive(2)
+        near_head(i)
         return 0
 
     lax.fori_loop(0, heads, step, 0)
-    for b in range(3, bits):
-        arrive(b)
 
     def rest(n, _):
         own = rows_of(head_chunk(n, 0, 0))
@@ -242,14 +250,12 @@
         return 0
 
     lax.fori_loop(heads // 4, heads, rest, 0)
-    for b in range(2, bits):
-        gather(b)
-
-    def far_head(h, _):
+
+    def far_head(h, chosen, last):
         where = rows_of(h)
         high = []
         low = []
-        for b in range(bits):
+        for b in chosen:
             full = jnp.where(bit[b] == 1, buckets[b, where, :], 0.0)
             top = full.astype(jnp.bfloat16)
             high.append(top)
@@ -259,16 +265,40 @@
             cols = pl.ds(ti * TILE, TILE)
             query = q_heads[h, cols, :]
             products = nt_dot(both, jnp.concatenate([query, query], 1))
-            far = None
-            for b in range(bits):
-                term = products[b * width : (b + 1) * width] * w_ref[h, pl.ds(local_bits + 1 + b, 1), cols]
-                far = term if far is None else far + term
-            total = near[h, :, cols] + far
-            scale = lax.rsqrt(jnp.mean(total * total, 0, keepdims=True) + EPSILON)
-            wide_b[pl.ds(ti * TILE * heads + h, TILE, stride=heads), :] = (total * scale).T
-        return 0
-
-    lax.fori_loop(0, heads, far_head, 0)
+            total = near[h, :, cols]
+            for n, b in enumerate(chosen):
+                total = total + products[n * width : (n + 1) * width] * w_in[h, pl.ds(local_bits + 1 + b, 1), cols]
+            if last:
+                scale = lax.rsqrt(jnp.mean(total * total, 0, keepdims=True) + EPSILON)
+                wide_b[pl.ds(ti * TILE * heads + h, TILE, stride=heads), :] = (total * scale).T
+            else:
+                near[h, :, cols] = total
+
+    def far_loop(chosen, last, events):
+        def one(h, _):
+            for at, work in events:
+                pl.when(h == at)(work)
+            far_head(h, chosen, last)
+            return 0
+        lax.fori_loop(0, heads, one, 0)
+
+    far_loop([0, 1], False, [(heads // 2, lambda: arrive(2))])
+    waits = [(b, 1 + len(key) + b, key) for b in range(3, bits) for key in [()] + subsets(split_of(b))]
+    waits += [(2, 4 + len(key), key) for key in subsets(split_of(2))]
+    waits.sort(key=lambda w: (w[1], w[0]))
+    early = max(n for n, w in enumerate(waits) if w[0] == 2) + 1
+
+    def work_of(b, key):
+        return (lambda: gather(b, key)) if key else (lambda: arrive(b))
+
+    work = [work_of(b, key) for b, _, key in waits]
+    for w in work[:early]:
+        w()
+    late = work[early:]
+    far_loop([2], False, [(1 + n * (heads - 1) // len(late), w) for n, w in enumerate(late[: len(late) // 2])])
+    for w in late[len(late) // 2 :]:
+        w()
+    far_loop(list(range(3, bits)), True, [])
 
     def narrow(i, _):
         at = pl.multiple_of(i * part, part)
@@ -306,13 +336,17 @@
     bits = short_bits + long_bits
     rows = heads * width
     copies = 2 * heads + sum(1 << min(b, short_bits) for b in range(2, bits))
-    vmem = pl.BlockSpec(memory_space=pltpu.VMEM)
+    level_weight = jnp.transpose(level_weight, (1, 0, 2))
     return pl.pallas_call(
         functools.partial(kernel, short_bits, long_bits, heads, length, width),
         out_shape=jax.ShapeDtypeStruct(query.shape, jnp.bfloat16),
-        in_specs=[vmem] * 4,
-        out_specs=vmem,
+        in_specs=[pl.BlockSpec(memory_space=pl.ANY)] * 4,
+        out_specs=pl.BlockSpec(memory_space=pltpu.VMEM),
         scratch_shapes=[
+            pltpu.VMEM(query.shape, jnp.bfloat16),
+            pltpu.VMEM(query.shape, jnp.bfloat16),
+            pltpu.VMEM(query.shape, jnp.bfloat16),
+            pltpu.VMEM((heads, level_weight.shape[0], length), jnp.float32),
             pltpu.VMEM((length * heads, width), jnp.float32),
             pltpu.VMEM((length * heads, width), jnp.float32),
             pltpu.VMEM((heads, length, width), jnp.bfloat16),
@@ -324,6 +358,7 @@
             pltpu.VMEM((bits, rows, width), jnp.float32),
             pltpu.SemaphoreType.DMA((copies,)),
             pltpu.SemaphoreType.DMA((copies,)),
+            pltpu.SemaphoreType.DMA((3 + heads,)),
         ],
         compiler_params=pltpu.CompilerParams(
             collective_id=0, has_side_effects=True, vmem_limit_bytes=60 * 1024 * 1024

time: 56.8 us -> 53.6 us (0.944)
  the two profiles are of different devices: /device:TPU:22 before, /device:TPU:2 now
where the time goes in v2:
time: 53.6 us; the launch traced here: 53.5 us
  Pallas kernels  50.4 us (94%)
  local copies, waits for them, and re-layouts  3.05 us (6%)
    pallas_call x1, Pallas kernels, per_device(): pl.pallas_call(functools.partial(kernel, short_bits, long_bits, heads, le...  50.4 us
    unnamed x1, local copies, waits for them, and re-layouts  3.05 us

profile of v2, /device:TPU:2, one launch (start us, length us, event | category | flops | bytes accessed | tf_op | source)
XLA Modules:
  0.0 53.5 jit_solution(12734114595377231957)
XLA Ops:
  0.0 50.4 %shard_map.46 = bf16[1024,8,128]{2,1,0:T(8,128)(2,1)} custom-call(bf16[1024,8,128]{2,1,0:T(8,128)(2,1)} %q_ref.1, bf16[1024,8,128]{2,1,0:T(8,128)(2,1)} %k_ref.1, bf16[1024,8,128]{2,1,0:T(8,128)(2,1)} %v_ref.1, f32[20,8,1024]{2,1,0:T(8,128)} %bitcast.1), custom_call_target="tpu_custom_call" | custom-call | tf_op jit(solution)/shard_map/pallas_call | solution.py:340
  50.4 3.0 %copy.6 = bf16[1024,8,128]{2,1,0:T(8,128)(2,1)} copy(bf16[1024,8,128]{2,1,0:T(8,128)(2,1)} %shard_map.46) | data formatting | bytes 4194304

commit v3 on v2

--- a/solution.py
+++ b/solution.py
@@ -24,11 +24,22 @@
 
 
 def subsets(bits):
-    found = []
-    for mask in range(1, 1 << len(bits)):
-        found.append(tuple(b for i, b in enumerate(bits) if mask >> i & 1))
-    found.sort(key=lambda s: (len(s), [-b for b in reversed(s)]))
-    return found
+    found = [tuple(b for i, b in enumerate(bits) if mask >> i & 1) for mask in range(1 << len(bits))]
+    return sorted(found, key=len)
+
+
+def runs_of(b, short_bits):
+    return subsets(list(range(b, short_bits)))
+
+
+def order_of(b, short_bits):
+    if b > short_bits:
+        return [short_bits] + list(range(short_bits))
+    return list(range(min(b, short_bits)))
+
+
+def pieces_of(b, short_bits):
+    return [(run, key) for run in runs_of(b, short_bits) for key in subsets(order_of(b, short_bits))]
 
 
 def nt_dot(a, b):
@@ -53,15 +64,14 @@
             return {"short": short_pos + (1 - 2 * bit[b]) * (1 << b)}
         return {"long": long_pos + (1 - 2 * bit[b]) * (1 << b - short_bits)}
 
-    def split_of(b):
-        return list(range(min(b, short_bits))) if b >= 2 else []
-
     def piece(b, flips):
-        split = split_of(b)
         start = 0
-        for i, s in enumerate(split):
-            start = start + (rows >> i + 1) * flipped(bit[s], 1 if s in flips else 0)
-        size = rows >> len(split)
+        for i in range(short_bits):
+            start = start + (rows >> i + 1) * flipped(bit[i], 1 if i in flips else 0)
+        size = rows >> short_bits
+        if b > short_bits:
+            size = size // 2
+            start = start + size * flipped(bit[short_bits], 1 if short_bits in flips else 0)
         return pl.ds(pl.multiple_of(start, 8), size)
 
     number = {}
@@ -69,8 +79,8 @@
         number[b] = b * heads
     count = 2 * heads
     for b in range(2, bits):
-        for key in [()] + subsets(split_of(b)):
-            number[b, key] = count
+        for run, key in pieces_of(b, short_bits):
+            number[b, run, key] = count
             count += 1
 
     def copy(src, dst, where, no, to):
@@ -186,44 +196,73 @@
                 total = product if total is None else total + product
             near[h, :, cols] = total
 
-    def received(b, key, where):
-        copy(sums.at[b], buckets.at[b], where, number[b, key], b if not key else key[0]).wait_recv()
+    def received(b, run, key):
+        copy(
+            sums.at[b], buckets.at[b], piece(b, run + key), number[b, run, key], key[0] if key else b
+        ).wait_recv()
 
     def add_up(b, where):
         sums[b + 1, where, :] = sums[b, where, :] + buckets[b, where, :]
 
-    def send_sums(b):
-        c = copy(sums.at[b], buckets.at[b], piece(b, ()), number[b, ()], b)
+    def sum_copy(b, run):
+        there = tuple(sorted(set(run) ^ {b})) if b < short_bits else run
+        return copy(sums.at[b], buckets.at[b], piece(b, run), number[b, there, ()], b)
+
+    def if_needed(b, do):
         if b < bits - 1:
-            c.start()
+            do()
         else:
-            pl.when(bit[b] == 0)(c.start)
-
-    def pass_on(b, key):
-        for g in split_of(b):
-            if not key or g < key[0]:
-                copy(buckets.at[b], buckets.at[b], piece(b, key), number[b, (g,) + key], g).start()
-
-    def arrive(b):
+            pl.when(bit[b] == 0)(do)
+
+    def shares(b, run, key):
+        order = order_of(b, short_bits)
+        upto = order.index(key[0]) if key else len(order)
+        return [
+            copy(buckets.at[b], buckets.at[b], piece(b, run + key), number[b, run, (g,) + key], g)
+            for g in reversed(order[:upto])
+        ]
+
+    def arrive(b, run):
         if b < bits - 1:
-            received(b, (), piece(b, ()))
-            add_up(b, piece(b + 1, ()))
-            send_sums(b + 1)
-
-            @pl.when(bit[b] == 1)
-            def _():
-                pass_on(b, ())
-        else:
-            @pl.when(bit[b] == 1)
-            def _():
-                received(b, (), piece(b, ()))
-                pass_on(b, ())
-
-    def gather(b, key):
+            received(b, run, ())
+            if b not in run:
+                add_up(b, piece(b, run))
+                if_needed(b + 1, lambda: sum_copy(b + 1, run).start())
+
         @pl.when(bit[b] == 1)
         def _():
-            received(b, key, piece(b, key))
-            pass_on(b, key)
+            if b == bits - 1:
+                received(b, run, ())
+            for c in shares(b, run, ()):
+                c.start()
+
+    def gather(b, run, key):
+        @pl.when(bit[b] == 1)
+        def _():
+            received(b, run, key)
+            for c in shares(b, run, key):
+                c.start()
+
+    def time_of(b, run, key):
+        base = 2 * (b - 2) + (2 if run else 0)
+        return base + 2 * len(key) + 0.1 * b
+
+    events = [(b, run, key) for b in range(2, bits) for run, key in pieces_of(b, short_bits)]
+    events.sort(key=lambda e: time_of(*e))
+    spot = max(n for n, e in enumerate(events) if e[0] < short_bits) + 1
+
+    def work_of(b, run, key):
+        return (lambda: gather(b, run, key)) if key else (lambda: arrive(b, run))
+
+    work = [work_of(*e) for e in events]
+    first = 2
+    middle = first + (spot - first) * 2 // 3
+    late = spot + (len(work) - spot) // 2
+
+    def spread(work, start, stop):
+        return [(start + n * (stop - start) // len(work), w) for n, w in enumerate(work)]
+
+    near_events = spread(work[:first], heads - 2, heads)
 
     def step(i, _):
         where = rows_of(head_chunk(i, 0, 1))
@@ -231,14 +270,17 @@
         add_up(0, where)
         copy(sums.at[1], buckets.at[1], where, number[1] + i, 1).start()
 
-        @pl.when(i == heads // 2)
+        @pl.when(i == heads // 4 + 1)
         def _():
             for n in range(heads // 4):
                 own = rows_of(head_chunk(n, 0, 0))
                 copy(sums.at[1], buckets.at[1], own, number[1] + n, 1).wait_recv()
-            add_up(1, piece(2, ()))
-            send_sums(2)
-
+                add_up(1, own)
+            for run in reversed(runs_of(2, short_bits)):
+                sum_copy(2, run).start()
+
+        for at, do in near_events:
+            pl.when(i == at)(do)
         near_head(i)
         return 0
 
@@ -276,29 +318,19 @@
 
     def far_loop(chosen, last, events):
         def one(h, _):
-            for at, work in events:
-                pl.when(h == at)(work)
+            for at, do in events:
+                pl.when(h == at)(do)
             far_head(h, chosen, last)
             return 0
         lax.fori_loop(0, heads, one, 0)
 
-    far_loop([0, 1], False, [(heads // 2, lambda: arrive(2))])
-    waits = [(b, 1 + len(key) + b, key) for b in range(3, bits) for key in [()] + subsets(split_of(b))]
-    waits += [(2, 4 + len(key), key) for key in subsets(split_of(2))]
-    waits.sort(key=lambda w: (w[1], w[0]))
-    early = max(n for n, w in enumerate(waits) if w[0] == 2) + 1
-
-    def work_of(b, key):
-        return (lambda: gather(b, key)) if key else (lambda: arrive(b))
-
-    work = [work_of(b, key) for b, _, key in waits]
-    for w in work[:early]:
-        w()
-    late = work[early:]
-    far_loop([2], False, [(1 + n * (heads - 1) // len(late), w) for n, w in enumerate(late[: len(late) // 2])])
-    for w in late[len(late) // 2 :]:
-        w()
-    far_loop(list(range(3, bits)), True, [])
+    far_loop([0, 1], False, spread(work[first:middle], 0, heads))
+    for do in work[middle:spot]:
+        do()
+    far_loop(list(range(2, short_bits)), False, spread(work[spot:late], 1, heads))
+    for do in work[late:]:
+        do()
+    far_loop(list(range(short_bits, bits)), True, [])
 
     def narrow(i, _):
         at = pl.multiple_of(i * part, part)
@@ -315,18 +347,14 @@
 
     lax.fori_loop(0, heads, sent, 0)
     for b in range(2, bits):
-        c = copy(sums.at[b], buckets.at[b], piece(b, ()), number[b, ()], b)
-        if b < bits - 1:
-            c.wait_send()
-        else:
-            pl.when(bit[b] == 0)(c.wait_send)
+        for run in runs_of(b, short_bits):
+            if_needed(b, lambda: sum_copy(b, run).wait_send())
 
         @pl.when(bit[b] == 1)
         def _():
-            for key in [()] + subsets(split_of(b)):
-                for g in split_of(b):
-                    if not key or g < key[0]:
-                        copy(buckets.at[b], buckets.at[b], piece(b, key), number[b, (g,) + key], g).wait_send()
+            for run, key in pieces_of(b, short_bits):
+                for c in shares(b, run, key):
+                    c.wait_send()
 
 
 def per_device(query, key, value, level_weight):
@@ -335,7 +363,7 @@
     long_bits = log2(lax.axis_size("long"))
     bits = short_bits + long_bits
     rows = heads * width
-    copies = 2 * heads + sum(1 << min(b, short_bits) for b in range(2, bits))
+    copies = 2 * heads + sum(len(pieces_of(b, short_bits)) for b in range(2, bits))
     level_weight = jnp.transpose(level_weight, (1, 0, 2))
     return pl.pallas_call(
         functools.partial(kernel, short_bits, long_bits, heads, length, width),

time: 53.6 us -> 53.4 us (level)
  the two profiles are of different devices: /device:TPU:2 before, /device:TPU:3 now
where the time goes in v3:
time: 53.4 us; the launch traced here: 53.2 us
  Pallas kernels  50.2 us (94%)
  local copies, waits for them, and re-layouts  3.05 us (6%)
    pallas_call x1, Pallas kernels, per_device(): pl.pallas_call(functools.partial(kernel, short_bits, long_bits, heads, le...  50.2 us
    unnamed x1, local copies, waits for them, and re-layouts  3.05 us

profile of v3, /device:TPU:3, one launch (start us, length us, event | category | flops | bytes accessed | tf_op | source)
XLA Modules:
  0.0 53.2 jit_solution(3717845300736350947)
XLA Ops:
  0.0 50.2 %shard_map.46 = bf16[1024,8,128]{2,1,0:T(8,128)(2,1)} custom-call(bf16[1024,8,128]{2,1,0:T(8,128)(2,1)} %q_ref.1, bf16[1024,8,128]{2,1,0:T(8,128)(2,1)} %k_ref.1, bf16[1024,8,128]{2,1,0:T(8,128)(2,1)} %v_ref.1, f32[20,8,1024]{2,1,0:T(8,128)} %bitcast.1), custom_call_target="tpu_custom_call" | custom-call | tf_op jit(solution)/shard_map/pallas_call | solution.py:368
  50.2 3.0 %copy.6 = bf16[1024,8,128]{2,1,0:T(8,128)(2,1)} copy(bf16[1024,8,128]{2,1,0:T(8,128)(2,1)} %shard_map.46) | data formatting | bytes 4194304

commit v4 on v3

--- a/solution.py
+++ b/solution.py
@@ -255,7 +255,7 @@
         return (lambda: gather(b, run, key)) if key else (lambda: arrive(b, run))
 
     work = [work_of(*e) for e in events]
-    first = 2
+    first = 4
     middle = first + (spot - first) * 2 // 3
     late = spot + (len(work) - spot) // 2
 

time: 53.4 us -> 52.9 us (level)
  no operation moved by 1% of the time
where the time goes in v4:
time: 52.9 us; the launch traced here: 52.8 us
  Pallas kernels  49.7 us (94%)
  local copies, waits for them, and re-layouts  3.05 us (6%)
    pallas_call x1, Pallas kernels, per_device(): pl.pallas_call(functools.partial(kernel, short_bits, long_bits, heads, le...  49.7 us
    unnamed x1, local copies, waits for them, and re-layouts  3.05 us

profile of v4, /device:TPU:3, one launch (start us, length us, event | category | flops | bytes accessed | tf_op | source)
XLA Modules:
  0.0 52.8 jit_solution(11511608346823124143)
XLA Ops:
  0.0 49.7 %shard_map.46 = bf16[1024,8,128]{2,1,0:T(8,128)(2,1)} custom-call(bf16[1024,8,128]{2,1,0:T(8,128)(2,1)} %q_ref.1, bf16[1024,8,128]{2,1,0:T(8,128)(2,1)} %k_ref.1, bf16[1024,8,128]{2,1,0:T(8,128)(2,1)} %v_ref.1, f32[20,8,1024]{2,1,0:T(8,128)} %bitcast.1), custom_call_target="tpu_custom_call" | custom-call | tf_op jit(solution)/shard_map/pallas_call | solution.py:368
  49.7 3.0 %copy.6 = bf16[1024,8,128]{2,1,0:T(8,128)(2,1)} copy(bf16[1024,8,128]{2,1,0:T(8,128)(2,1)} %shard_map.46) | data formatting | bytes 4194304
